TPU v7x, 32 devices: a whole 2x2x4 slice. The times are simulated.
32 devices in a mesh: dp: 8 (over z, y), mp: 4 (over x, core).
Axes of the slice: x: 2, y: 2, z: 4, core: 2. Of those that a mesh axis runs over, the one named last changes fastest.
Arguments:
- tokens: bfloat16 [8192, 1024], P('dp'), may hold values from -6 to 6
- doc_lengths: int32 [8], P('dp'), may hold values from 256 to 1024, as said below
- cls_pos: int32 [8, 4], P('dp'), may hold values from 0 to 1023, as said below
- cls_count: int32 [8], P('dp'), may hold values from 1 to 4, as said below
- q_weight: bfloat16 [1024, 1024], P(None, 'mp'), may hold values from -0.1875 to 0.1875
- q_bias: bfloat16 [1024], P('mp'), may hold values from -2 to 2
- k_weight: bfloat16 [1024, 1024], P(None, 'mp'), may hold values from -0.1875 to 0.1875
- v_weight: bfloat16 [1024, 1024], P(None, 'mp'), may hold values from -0.1875 to 0.1875
- v_bias: bfloat16 [1024], P('mp'), may hold values from -2 to 2
- o_weight: bfloat16 [1024, 1024], P('mp'), may hold values from -1.5 to 1.5
- o_bias: bfloat16 [1024], replicated, may hold values from -2 to 2
- ln1_gain: bfloat16 [1024], replicated, may hold values from 0.5 to 1.5
- ln1_bias: bfloat16 [1024], replicated, may hold values from -2 to 2
- up_weight: bfloat16 [1024, 4096], P(None, 'mp'), may hold values from -0.1875 to 0.1875
- up_bias: bfloat16 [4096], P('mp'), may hold values from -2 to 2
- down_weight: bfloat16 [4096, 1024], P('mp'), may hold values from -0.09375 to 0.09375
- down_bias: bfloat16 [1024], replicated, may hold values from -2 to 2
- ln2_gain: bfloat16 [1024], replicated, may hold values from 0.5 to 1.5
- ln2_bias: bfloat16 [1024], replicated, may hold values from -2 to 2
- out_grad: bfloat16 [8192, 1024], P('dp'), may hold values from -6 to 6
- pooled_grad: float32 [8, 4, 1024], P('dp'), may hold values from -6 to 6
Outputs:
- out: bfloat16 [8192, 1024], P('dp')
- pooled: float32 [8, 4, 1024], P('dp')
- in_grad: float32 [8192, 1024], P('dp')
- q_weight_grad: float32 [1024, 1024], P('dp', 'mp')
- q_bias_grad: float32 [1024], P('mp')
- k_weight_grad: float32 [1024, 1024], P('dp', 'mp')
- v_weight_grad: float32 [1024, 1024], P('dp', 'mp')
- v_bias_grad: float32 [1024], P('mp')
- o_weight_grad: float32 [1024, 1024], P('mp', 'dp')
- o_bias_grad: float32 [1024], replicated
- ln1_gain_grad: float32 [1024], replicated
- ln1_bias_grad: float32 [1024], replicated
- up_weight_grad: float32 [1024, 4096], P('dp', 'mp')
- up_bias_grad: float32 [4096], P('mp')
- down_weight_grad: float32 [4096, 1024], P('mp', 'dp')
- down_bias_grad: float32 [1024], replicated
- ln2_gain_grad: float32 [1024], replicated
- ln2_bias_grad: float32 [1024], replicated
Inputs may be any that keep to these rules, and one draw needn't show every extreme that they name: `doc_lengths`: in every draw some document fills all 1024 slots. `cls_count`: A document's length divided by 256, rounded up; some document has 4. `cls_pos`: for j below the document's cls_count, entry j lies in [j * 256, (j + 1) * 256) and below the document's length; later entries are 0. In a document of 1024 tokens the last entry is 1023.
All inputs are finite; a program needn't handle non-finite values.
Results may differ from a plain program's by a relative error of at most 0.014.
The roundings to bfloat16 on the way count: a program that leaves them out, or rounds other values in their place, can miss the bound.
Values sent between devices are 32-bit elements; how exact they have to be, the bound alone decides.
No kernel may reach another device: no remote copies, remote signals or barrier semaphores. Data moves between devices by JAX's collectives and lax.ppermute only.
A program may use at most 128 MiB of HBM per device.

v0:
```python
import jax
import jax.numpy as jnp
from jax import lax
from jax.sharding import PartitionSpec as P

HEAD_DIM = 64
BLOCK = 512


norm_eps = 1e-05
highest = lax.Precision.HIGHEST
root_half = 0.7071067811865476
inv_root_tau = 0.3989422804014327


def contract_rows(left_side, right_side):
    return lax.dot_general(
        left_side, right_side, (((0,), (0,)), ((), ())), preferred_element_type=jnp.float32
    )


def contract_cols(left_side, right_side):
    return lax.dot_general(
        left_side, right_side, (((1,), (1,)), ((), ())), preferred_element_type=jnp.float32
    )


def norm_parts(values, gain_vec, shift_vec):
    centre = values - jnp.mean(values, axis=-1, keepdims=True)
    spread = jnp.mean(centre * centre, axis=-1, keepdims=True)
    scale_inv = lax.rsqrt(spread + norm_eps)
    unit_rows = centre * scale_inv
    return (unit_rows * gain_vec + shift_vec, unit_rows, scale_inv)


def norm_back(grad_rows, unit_rows, scale_inv, gain_vec):
    scaled = grad_rows * gain_vec
    inner = (
        scaled
        - jnp.mean(scaled, axis=-1, keepdims=True)
        - unit_rows * jnp.mean(scaled * unit_rows, axis=-1, keepdims=True)
    )
    return (scale_inv * inner, jnp.sum(grad_rows * unit_rows, axis=0), jnp.sum(grad_rows, axis=0))


def shards(
    tokens,
    doc_lengths,
    cls_pos,
    cls_count,
    q_weight,
    q_bias,
    k_weight,
    v_weight,
    v_bias,
    o_weight,
    o_bias,
    ln1_gain,
    ln1_bias,
    up_weight,
    up_bias,
    down_weight,
    down_bias,
    ln2_gain,
    ln2_bias,
    out_grad,
    pooled_grad,
):
    slot_len = tokens.shape[0]
    local_heads = q_weight.shape[1] // HEAD_DIM
    blocks = slot_len // BLOCK
    length = doc_lengths[0]
    keep_mask = lax.iota(jnp.int32, slot_len) < length
    keep_rows = keep_mask.astype(jnp.float32)[:, None]
    inputs_full = tokens.astype(jnp.float32)
    head_shape = (slot_len, local_heads, HEAD_DIM)
    queries = (
        (jnp.dot(tokens, q_weight, preferred_element_type=jnp.float32) + q_bias.astype(jnp.float32))
        .astype(jnp.bfloat16)
        .reshape(head_shape)
    )
    key_rows = (
        jnp.dot(tokens, k_weight, preferred_element_type=jnp.float32)
        .astype(jnp.bfloat16)
        .reshape(head_shape)
    )
    value_rows = (
        (jnp.dot(tokens, v_weight, preferred_element_type=jnp.float32) + v_bias.astype(jnp.float32))
        .astype(jnp.bfloat16)
        .reshape(head_shape)
    )

    def block_scores(row_start):
        query_block = lax.dynamic_slice_in_dim(queries, row_start, BLOCK, 0)
        raw_scores = (
            jnp.einsum("qhd,khd->hqk", query_block, key_rows, preferred_element_type=jnp.float32)
            * 0.125
        )
        return (query_block, jnp.where(keep_mask[None, None, :], raw_scores, -1e30))

    def forward_block(block_index):
        row_start = block_index * BLOCK
        query_block, scores = block_scores(row_start)
        row_top = jnp.max(scores, axis=-1, keepdims=True)
        exp_scores = jnp.exp(scores - row_top)
        row_total = jnp.sum(exp_scores, axis=-1, keepdims=True)
        probs_low = (exp_scores / row_total).astype(jnp.bfloat16)
        context = jnp.einsum(
            "hqk,khd->qhd", probs_low, value_rows, preferred_element_type=jnp.float32
        )
        return (context, (row_top + jnp.log(row_total))[..., 0])

    contexts, log_totals = lax.map(forward_block, jnp.arange(blocks))
    context_low = contexts.reshape(slot_len, -1).astype(jnp.bfloat16)
    attended = lax.psum(
        jnp.dot(context_low, o_weight, preferred_element_type=jnp.float32), "mp"
    ) + o_bias.astype(jnp.float32)
    gain_one = ln1_gain.astype(jnp.float32)
    gain_two = ln2_gain.astype(jnp.float32)
    normed, unit_one, inv_one = norm_parts(
        inputs_full + attended, gain_one, ln1_bias.astype(jnp.float32)
    )
    normed_low = normed.astype(jnp.bfloat16)
    pre_active = jnp.dot(
        normed_low, up_weight, preferred_element_type=jnp.float32
    ) + up_bias.astype(jnp.float32)
    active_low = jax.nn.gelu(pre_active, approximate=False).astype(jnp.bfloat16)
    fed_rows = lax.psum(
        jnp.dot(active_low, down_weight, preferred_element_type=jnp.float32), "mp"
    ) + down_bias.astype(jnp.float32)
    out_pre, unit_two, inv_two = norm_parts(
        normed + fed_rows, gain_two, ln2_bias.astype(jnp.float32)
    )
    out_rows = out_pre * keep_rows
    slot_ids = lax.iota(jnp.int32, cls_pos.shape[1])
    picker = (
        (cls_pos[0][:, None] == lax.iota(jnp.int32, slot_len)[None, :])
        & (slot_ids < cls_count[0])[:, None]
    ).astype(jnp.float32)
    pooled = jnp.dot(picker, out_rows, precision=highest)[None]
    placed = lax.dot_general(picker, pooled_grad[0], (((0,), (0,)), ((), ())), precision=highest)
    grad_out = (out_grad.astype(jnp.float32) + placed) * keep_rows
    grad_two, ln2_gain_grad, ln2_bias_grad = norm_back(grad_out, unit_two, inv_two, gain_two)
    grad_fed = grad_two.astype(jnp.bfloat16)
    down_bias_grad = jnp.sum(grad_fed.astype(jnp.float32), axis=0)
    down_weight_grad = contract_rows(active_low, grad_fed)
    grad_active = contract_cols(grad_fed, down_weight)
    normal_cdf = 0.5 * (1.0 + jax.scipy.special.erf(pre_active * root_half))
    density = jnp.exp(-0.5 * pre_active * pre_active) * inv_root_tau
    grad_pre = (grad_active * (normal_cdf + pre_active * density)).astype(jnp.bfloat16)
    up_bias_grad = jnp.sum(grad_pre.astype(jnp.float32), axis=0)
    up_weight_grad = contract_rows(normed_low, grad_pre)
    ffn_pair = (up_weight_grad, down_weight_grad)
    grad_normed = grad_two + lax.psum(contract_cols(grad_pre, up_weight), "mp")
    grad_first, ln1_gain_grad, ln1_bias_grad = norm_back(grad_normed, unit_one, inv_one, gain_one)
    grad_attended = grad_first.astype(jnp.bfloat16)
    o_bias_grad = jnp.sum(grad_attended.astype(jnp.float32), axis=0)
    o_weight_grad = contract_rows(context_low, grad_attended)
    grad_context = contract_cols(grad_attended, o_weight).astype(jnp.bfloat16).reshape(head_shape)
    zero_heads = jnp.zeros(head_shape, jnp.float32)

    def backward_block(carried, block_index):
        row_start = block_index * BLOCK
        key_sum, value_sum = carried
        query_block, scores = block_scores(row_start)
        log_block = log_totals[block_index]
        soft_probs = jnp.exp(scores - log_block[..., None])
        probs_low = soft_probs.astype(jnp.bfloat16)
        grad_block = lax.dynamic_slice_in_dim(grad_context, row_start, BLOCK, 0)
        grad_probs = jnp.einsum(
            "qhd,khd->hqk", grad_block, value_rows, preferred_element_type=jnp.float32
        )
        row_inner = jnp.sum(soft_probs * grad_probs, axis=-1, keepdims=True)
        grad_scores = (soft_probs * (grad_probs - row_inner)).astype(jnp.bfloat16)
        grad_query = (
            jnp.einsum("hqk,khd->qhd", grad_scores, key_rows, preferred_element_type=jnp.float32)
            * 0.125
        )
        key_sum = (
            key_sum
            + jnp.einsum(
                "hqk,qhd->khd", grad_scores, query_block, preferred_element_type=jnp.float32
            )
            * 0.125
        )
        value_sum = value_sum + jnp.einsum(
            "hqk,qhd->khd", probs_low, grad_block, preferred_element_type=jnp.float32
        )
        return ((key_sum, value_sum), grad_query)

    (key_grads, value_grads), query_grads = lax.scan(
        backward_block, (zero_heads, zero_heads), jnp.arange(blocks)
    )
    grad_queries = query_grads.reshape(slot_len, -1).astype(jnp.bfloat16)
    grad_keys = key_grads.reshape(slot_len, -1).astype(jnp.bfloat16)
    grad_values = value_grads.reshape(slot_len, -1).astype(jnp.bfloat16)
    q_bias_grad = jnp.sum(grad_queries.astype(jnp.float32), axis=0)
    v_bias_grad = jnp.sum(grad_values.astype(jnp.float32), axis=0)
    q_weight_grad = contract_rows(tokens, grad_queries)
    k_weight_grad = contract_rows(tokens, grad_keys)
    v_weight_grad = contract_rows(tokens, grad_values)
    input_part = (
        contract_cols(grad_queries, q_weight)
        + contract_cols(grad_keys, k_weight)
        + contract_cols(grad_values, v_weight)
    )
    in_grad = grad_first + lax.psum(input_part, "mp")
    q_sum, k_sum, v_sum, o_sum, up_sum, down_sum = (
        lax.psum_scatter(q_weight_grad, "dp", scatter_dimension=0, tiled=True),
        lax.psum_scatter(k_weight_grad, "dp", scatter_dimension=0, tiled=True),
        lax.psum_scatter(v_weight_grad, "dp", scatter_dimension=0, tiled=True),
        lax.psum_scatter(o_weight_grad, "dp", scatter_dimension=1, tiled=True),
        lax.psum_scatter(ffn_pair[0], "dp", scatter_dimension=0, tiled=True),
        lax.psum_scatter(ffn_pair[1], "dp", scatter_dimension=1, tiled=True),
    )
    small_sums = lax.psum(
        (
            q_bias_grad,
            v_bias_grad,
            o_bias_grad,
            ln1_gain_grad,
            ln1_bias_grad,
            up_bias_grad,
            down_bias_grad,
            ln2_gain_grad,
            ln2_bias_grad,
        ),
        "dp",
    )
    return (
        out_rows.astype(jnp.bfloat16),
        pooled,
        in_grad,
        q_sum,
        small_sums[0],
        k_sum,
        v_sum,
        small_sums[1],
        o_sum,
        small_sums[2],
        small_sums[3],
        small_sums[4],
        up_sum,
        small_sums[5],
        down_sum,
        small_sums[6],
        small_sums[7],
        small_sums[8],
    )


def solution(mesh):
    return jax.shard_map(
        shards,
        mesh=mesh,
        in_specs=(
            P("dp", None),
            P("dp"),
            P("dp", None),
            P("dp"),
            P(None, "mp"),
            P("mp"),
            P(None, "mp"),
            P(None, "mp"),
            P("mp"),
            P("mp", None),
            P(),
            P(),
            P(),
            P(None, "mp"),
            P("mp"),
            P("mp", None),
            P(),
            P(),
            P(),
            P("dp", None),
            P("dp", None, None),
        ),
        out_specs=(
            P("dp", None),
            P("dp", None, None),
            P("dp", None),
            P("dp", "mp"),
            P("mp"),
            P("dp", "mp"),
            P("dp", "mp"),
            P("mp"),
            P("mp", "dp"),
            P(),
            P(),
            P(),
            P("dp", "mp"),
            P("mp"),
            P("mp", "dp"),
            P(),
            P(),
            P(),
        ),
        check_vma=False,
    )
```

profile of v0, /device:TPU:0, one launch (start us, length us, event | category | flops | bytes accessed | tf_op | source)
XLA Modules:
  0.0 936.6 jit_solution(439739643940356430)
XLA Ops:
  11.3 3.2 fusion.65
  16.1 17.3 %while.28 = (s32[]{:T(128)}, bf16[2,512,4,64]{1,3,2,0:T(8,128)(2,1)}, f32[2,4,512]{2,1,0:T(4,128)S(1)}, s32[2]{0:T(128)S(1)}, bf16[1024,4,64]{0,2,1:T(8,128)(2,1...) while((s32[]{:T(128)}, ...), condition=%wide.region_3.4_spmd.clone, body=%wide.region_0.3_spmd.clone.sunk | while | flops 562035712 | bytes 33362204 | solution.py:113
  36.0 3.8 fusion.88
  40.5 87.6 %all-reduce.6.cloned.1.call-done = f32[1024,1024]{1,0:T(8,128)} async-done(((f32[1024,1024]{1,0:T(8,128)}), f32[1024,1024]{1,0:T(8,128)}) %all-reduce.6.cloned.1.call-update) | async-done | bytes 4194320 | tf_op jit(solution)/shard_map/psum | solution.py:115
  128.1 3.5 fusion.87
  132.2 13.0 %fusion.42 = (bf16[1024,1024]{1,0:T(8,128)(2,1)S(1)}, f32[1024,1024]{1,0:T(8,128)}) fusion(f32[1024]{0:T(1024)S(1)} %convert_element_type.135, bf16[1024,1024]{1,0:T(8,128)(2,1)S(1)} %copy-done, f32[1024,1024]{1,0:T(8,128)S(1)} %get-tuple-element.284, f32[1024]{0:T(1024)S(1)} %convert_element_type.133, f32[1024]{0:T(1024)S(1)} %convert_element_type.132, ...), kind=kOutput, calls=%fused_computation.49 | convolution fusion | flops 2221932544 | bytes 12603392 | tf_op jit(solution)/shard_map/dot_general | solution.py:124
  146.6 4.3 fusion.89
  152.7 84.1 %all-reduce.8.cloned.1.call-done = f32[1024,1024]{1,0:T(8,128)} async-done(((f32[1024,1024]{1,0:T(8,128)}), f32[1024,1024]{1,0:T(8,128)}) %all-reduce.8.cloned.1.call-update) | async-done | bytes 4194320 | tf_op jit(solution)/shard_map/psum | solution.py:128
  236.8 4.3 fusion.86
  244.2 4.5 multiply_reduce_fusion.1
  248.8 3.6 convert_reduce_fusion
  252.4 4.2 convert_reduce_fusion.1
  257.9 4.4 fusion.90
  262.8 85.3 %all-reduce.10.cloned.1.call-done = f32[1024,1024]{1,0:T(8,128)} async-done(((f32[1024,1024]{1,0:T(8,128)}), f32[1024,1024]{1,0:T(8,128)}) %all-reduce.10.cloned.1.call-update) | async-done | bytes 4194320 | tf_op jit(solution)/shard_map/psum | solution.py:154
  348.1 6.1 multiply_reduce_fusion.2
  359.3 29.2 %while.29 = (s32[]{:T(128)}, f32[1024,4,64]{0,2,1:T(8,128)S(1)}, f32[1024,4,64]{0,2,1:T(8,128)}, bf16[2,512,4,64]{1,3,2,0:T(8,128)(2,1)}, s32[2]{0:T(128)S(1)}, ...) while((s32[]{:T(128)}, f32[1024,4,64]{0,2,1:T(8,128)S(1)}, ...), condition=%wide.region_17.18_spmd.clone, body=%wide.region_15.17_spmd.clone.sunk | while | flops 1375075328 | bytes 82899344 | solution.py:191
  389.9 3.3 convolution_bitcast_fusion
  394.1 3.3 convolution_bitcast_fusion.2
  397.6 3.3 convolution_bitcast_fusion.1
  403.7 2.7 add_add_fusion
  407.4 3.9 fusion.76
  411.4 7.3 fusion.79
  420.3 6.8 fusion.82
  427.9 4.6 fusion.66
  432.8 37.8 %all-reduce = (f32[256]{0:T(256)}, f32[256]{0:T(256)}, f32[1024]{0:T(1024)}, f32[1024]{0:T(1024)}, f32[1024]{0:T(1024)}, /*index=5*/f32[1024]{0:T(1024)}, f32[1024]{0:T(1024)}, f32[1024]{0:T(1024)}, f32[1024]{0:T(1024)}) all-reduce(f32[256]{0:T(256)S(1)} %reduce_sum.184, ...), channel_id=1, replica_groups=mesh['dp'=8,'mp'=4] {'dp'}, use_global_device_ids=true, to_apply=%region_21.22 | all-reduce | flops 7680 | bytes 61440 | tf_op jit(solution)/shard_map/psum | solution.py:216
  472.3 51.4 %reduce-scatter.7.cloned.1.call-done = f32[128,256]{0,1:T(8,128)} async-done(((f32[1024,256]{0,1:T(8,128)}), f32[128,256]{0,1:T(8,128)}) %reduce-scatter.7.cloned.1.call-update) | async-done | bytes 131088 | tf_op jit(solution)/shard_map/reduce_scatter | solution.py:209
  525.3 65.0 %reduce-scatter.9.cloned.1.call-done = f32[128,256]{0,1:T(8,128)} async-done(((f32[1024,256]{0,1:T(8,128)}), f32[128,256]{0,1:T(8,128)}) %reduce-scatter.9.cloned.1.call-update) | async-done | bytes 131088 | tf_op jit(solution)/shard_map/reduce_scatter | solution.py:210
  592.1 85.1 %all-reduce.12.cloned.1.call-done = f32[1024,1024]{1,0:T(8,128)} async-done(((f32[1024,1024]{1,0:T(8,128)}), f32[1024,1024]{1,0:T(8,128)}) %all-reduce.12.cloned.1.call-update) | async-done | bytes 4194320 | tf_op jit(solution)/shard_map/psum | solution.py:207
  677.2 6.8 add.198
  684.1 61.6 %reduce-scatter.13.cloned.1.call-done = f32[256,128]{1,0:T(8,128)} async-done(((f32[256,1024]{1,0:T(8,128)}), f32[256,128]{1,0:T(8,128)}) %reduce-scatter.13.cloned.1.call-update) | async-done | bytes 131088 | tf_op jit(solution)/shard_map/reduce_scatter | solution.py:212
  745.7 91.7 %reduce-scatter.17.cloned.1.call-done = f32[1024,128]{1,0:T(8,128)} async-done(((f32[1024,1024]{1,0:T(8,128)}), f32[1024,128]{1,0:T(8,128)}) %reduce-scatter.17.cloned.1.call-update) | async-done | bytes 524304 | tf_op jit(solution)/shard_map/reduce_scatter | solution.py:214
  837.4 92.2 %reduce-scatter.15.cloned.1.call-done = f32[128,1024]{1,0:T(8,128)} async-done(((f32[1024,1024]{1,0:T(8,128)}), f32[128,1024]{1,0:T(8,128)}) %reduce-scatter.15.cloned.1.call-update) | async-done | bytes 524304 | tf_op jit(solution)/shard_map/reduce_scatter | solution.py:213
  (224 shorter events, 74.6 us)
Async XLA Ops:
  7.2 125.0 %copy-start = (bf16[1024,1024]{1,0:T(8,128)(2,1)S(1)}, bf16[1024,1024]{1,0:T(8,128)(2,1)}, u32[]{:S(2)}) copy-start(bf16[1024,1024]{1,0:T(8,128)(2,1)} %param.38) | copy-start | bytes 6291460
  7.2 120.9 %all-reduce.6.cloned.1.call-start = ((), (), s32[]{:S(2)}) async-start(), calls=%async_computation.6 | async-start | bytes 8388608 | tf_op jit(solution)/shard_map/psum | solution.py:115
  7.3 7.3 copy-start.6
  7.3 7.3 copy-start.20
  39.8 197.0 %all-reduce.8.cloned.1.call-start = ((), (), s32[]{:S(2)}) async-start(), calls=%async_computation.7 | async-start | bytes 8388608 | tf_op jit(solution)/shard_map/psum | solution.py:128
  40.5 196.3 %copy-start.26 = (f32[1024]{0:T(1024)}, f32[1024]{0:T(1024)S(1)}, u32[]{:S(2)}) copy-start(f32[1024]{0:T(1024)S(1)} %convert_element_type.133) | copy-start | bytes 12292
  131.6 13.6 %copy-start.2 = (f32[1024,1024]{1,0:T(8,128)}, f32[1024,1024]{1,0:T(8,128)S(1)}, u32[]{:S(2)}) copy-start(f32[1024,1024]{1,0:T(8,128)S(1)} %get-tuple-element.284) | copy-start | bytes 12582916
  132.2 14.4 %copy-start.46 = (bf16[1024,1024]{1,0:T(8,128)(2,1)S(1)}, bf16[1024,1024]{1,0:T(8,128)(2,1)}, u32[]{:S(2)}) copy-start(bf16[1024,1024]{1,0:T(8,128)(2,1)} %param.40) | copy-start | bytes 6291460
  151.0 197.1 %all-reduce.10.cloned.1.call-start = ((), (), s32[]{:S(2)}) async-start(), calls=%async_computation.8 | async-start | bytes 8388608 | tf_op jit(solution)/shard_map/psum | solution.py:154
  152.6 96.1 %copy-start.28 = (f32[1024]{0:T(1024)}, f32[1024]{0:T(1024)S(1)}, u32[]{:S(2)}) copy-start(f32[1024]{0:T(1024)S(1)} %convert_element_type.138) | copy-start | bytes 12292
  152.6 96.1 %copy-start.30 = (f32[1024]{0:T(1024)}, f32[1024]{0:T(1024)S(1)}, u32[]{:S(2)}) copy-start(f32[1024]{0:T(1024)S(1)} %convert_element_type.139) | copy-start | bytes 12292
  152.6 89.1 %copy-start.51 = (pred[4]{0:T(512)(128)(4,1)}, pred[4]{0:T(512)(128)(4,1)S(1)}, u32[]{:S(2)}) copy-start(pred[4]{0:T(512)(128)(4,1)S(1)} %iota_compare_fusion.4) | copy-start | bytes 16
  152.6 96.0 %copy-start.32 = (f32[1024]{0:T(1024)}, f32[1024]{0:T(1024)S(1)}, u32[]{:S(2)}) copy-start(f32[1024]{0:T(1024)S(1)} %fusion.75) | copy-start | bytes 12292
  241.1 7.7 copy-start.5
  241.1 7.6 copy-start.23
  241.7 7.0 copy-start.34
  248.7 3.6 copy-start.47
  252.4 4.2 copy-start.7
  262.3 208.3 %reduce-scatter.11.cloned.1.call-start = ((), (), s32[]{:S(2)}) async-start(), calls=%async_computation.12 | async-start | bytes 1179648 | tf_op jit(solution)/shard_map/reduce_scatter | solution.py:211
  348.1 6.2 copy-start.3
  388.5 5.0 copy-start.14
  393.2 130.5 %reduce-scatter.7.cloned.1.call-start = ((), (), s32[]{:S(2)}) async-start(), calls=%async_computation.10 | async-start | bytes 1179648 | tf_op jit(solution)/shard_map/reduce_scatter | solution.py:209
  397.4 192.9 %reduce-scatter.9.cloned.1.call-start = ((), (), s32[]{:S(2)}) async-start(), calls=%async_computation.11 | async-start | bytes 1179648 | tf_op jit(solution)/shard_map/reduce_scatter | solution.py:210
  397.6 5.3 copy-start.21
  401.0 276.3 %all-reduce.12.cloned.1.call-start = ((), (), s32[]{:S(2)}) async-start(), calls=%async_computation.9 | async-start | bytes 8388608 | tf_op jit(solution)/shard_map/psum | solution.py:207
  406.4 339.3 %reduce-scatter.13.cloned.1.call-start = ((), (), s32[]{:S(2)}) async-start(), calls=%async_computation.13 | async-start | bytes 1179648 | tf_op jit(solution)/shard_map/reduce_scatter | solution.py:212
  411.4 426.0 %reduce-scatter.17.cloned.1.call-start = ((), (), s32[]{:S(2)}) async-start(), calls=%async_computation.15 | async-start | bytes 4718592 | tf_op jit(solution)/shard_map/reduce_scatter | solution.py:214
  418.7 510.8 %reduce-scatter.15.cloned.1.call-start = ((), (), s32[]{:S(2)}) async-start(), calls=%async_computation.14 | async-start | bytes 4718592 | tf_op jit(solution)/shard_map/reduce_scatter | solution.py:213
  427.8 5.0 copy-start.25
  427.9 5.0 copy-start.36
  427.9 5.0 copy-start.37
  590.3 339.2 %copy-start.1 = (bf16[1024,1024]{1,0:T(8,128)(2,1)S(1)}, bf16[1024,1024]{1,0:T(8,128)(2,1)}, u32[]{:S(2)}) copy-start(bf16[1024,1024]{1,0:T(8,128)(2,1)} %param.38) | copy-start | bytes 6291460
  (42 other events, 68.5 us)
Sparse Core Ops, SparseCore 0:
  39.9 88.1 all-reduce.5
  151.1 85.6 all-reduce.7
  262.4 85.6 all-reduce.9
  393.3 64.1 reduce-scatter.10
  460.8 62.8 reduce-scatter.6
  527.3 62.9 reduce-scatter.8
  592.7 84.5 all-reduce.11
  681.6 64.0 reduce-scatter.12
  749.9 87.4 reduce-scatter.16
  841.9 87.6 reduce-scatter.14
where the time goes:
time: 943 us; the launch traced here: 937 us
  waiting for transfers between devices  704 us (75%)
  matrix products  104 us (11%)
  other arithmetic  41.3 us (4%)
  blocking collectives  37.8 us (4%)
  local copies, waits for them, and re-layouts  25 us (3%)
  between operations  16.3 us (2%)
    reduce_scatter x1, waiting for transfers between devices, shards(): lax.psum_scatter(ffn_pair[0], 'dp', scatter_dimension=0, tiled=True)  92.2 us
    reduce_scatter x1, waiting for transfers between devices, shards(): lax.psum_scatter(ffn_pair[1], 'dp', scatter_dimension=1, tiled=True)  91.7 us
    psum x1, waiting for transfers between devices, shards(): lax.psum(jnp.dot(context_low, o_weight, preferred_element_type=jnp.float3...  87.6 us
    psum x1, waiting for transfers between devices, shards(): grad_normed = grad_two + lax.psum(contract_cols(grad_pre, up_weight), 'mp')  85.3 us
    psum x1, waiting for transfers between devices, shards(): in_grad = grad_first + lax.psum(input_part, 'mp')  85.1 us
    psum x1, waiting for transfers between devices, shards(): lax.psum(jnp.dot(active_low, down_weight, preferred_element_type=jnp.floa...  84.1 us
    reduce_scatter x1, waiting for transfers between devices, shards(): lax.psum_scatter(k_weight_grad, 'dp', scatter_dimension=0, tiled=True)  65 us
    reduce_scatter x1, waiting for transfers between devices, shards(): lax.psum_scatter(o_weight_grad, 'dp', scatter_dimension=1, tiled=True)  61.6 us
  transfers between devices with their start and end apart: 10, of which 9 were waited for; matrix products, arithmetic and copies ran while one was open for 5% of the time, Pallas kernels for 0%

commit v1 on v0

v1 whole, which is shorter than its diff:
```python
import functools

import jax
import jax.numpy as jnp
from jax import lax
from jax.experimental import pallas as pl
from jax.experimental.pallas import tpu as pltpu
from jax.sharding import PartitionSpec as P

HEAD_DIM = 64
NORM_EPS = 1e-05
ROOT_HALF = 0.7071067811865476
INV_ROOT_TAU = 0.3989422804014327
LOG2E = 1.4426950408889634
SCORE_SCALE = 0.125 * LOG2E
MASKED = -1e30

f32 = jnp.float32
bf16 = jnp.bfloat16
VMEM_LIMIT = 48 * 1024 * 1024


def dot_nn(a, b):
    return lax.dot_general(a, b, (((1,), (0,)), ((), ())), preferred_element_type=f32)


def dot_nt(a, b):
    return lax.dot_general(a, b, (((1,), (1,)), ((), ())), preferred_element_type=f32)


def dot_tn(a, b):
    return lax.dot_general(a, b, (((0,), (0,)), ((), ())), preferred_element_type=f32)


def attn_fwd_kernel(q_ref, k_ref, v_ref, bias_ref, o_ref, lse_ref):
    rows, width = q_ref.shape
    heads = width // HEAD_DIM
    lane = lax.broadcasted_iota(jnp.int32, (1, width), 1) // HEAD_DIM
    lse_lane = lax.broadcasted_iota(jnp.int32, (1, 128), 1)
    q = q_ref[...]
    k = k_ref[...]
    v = v_ref[...]
    bias = bias_ref[...]
    out = jnp.zeros((rows, width), f32)
    lse = jnp.zeros((rows, 128), f32)
    for h in range(heads):
        qh = jnp.where(lane == h, q, jnp.zeros_like(q))
        s = dot_nt(qh, k) * SCORE_SCALE + bias
        top = jnp.max(s, axis=1, keepdims=True)
        e = jnp.exp2(s - top)
        total = jnp.sum(e, axis=1, keepdims=True)
        p = (e * (1.0 / total)).astype(bf16)
        c = dot_nn(p, v)
        out = jnp.where(lane == h, c, out)
        lse = jnp.where(lse_lane == h, top + jnp.log2(total), lse)
    o_ref[...] = out.astype(o_ref.dtype)
    lse_ref[...] = lse


def attn_fwd(q, k, v, bias, block, dtype):
    rows, width = q.shape
    keys = k.shape[0]
    full = pl.BlockSpec((keys, width), lambda i: (0, 0))
    return pl.pallas_call(
        attn_fwd_kernel,
        grid=(rows // block,),
        in_specs=[
            pl.BlockSpec((block, width), lambda i: (i, 0)),
            full,
            full,
            pl.BlockSpec((1, keys), lambda i: (0, 0)),
        ],
        out_specs=[
            pl.BlockSpec((block, width), lambda i: (i, 0)),
            pl.BlockSpec((block, 128), lambda i: (i, 0)),
        ],
        out_shape=[
            jax.ShapeDtypeStruct((rows, width), dtype),
            jax.ShapeDtypeStruct((rows, 128), f32),
        ],
        compiler_params=pltpu.CompilerParams(vmem_limit_bytes=VMEM_LIMIT),
        cost_estimate=pl.CostEstimate(
            flops=4 * rows * keys * width * (width // HEAD_DIM),
            bytes_accessed=4 * keys * width + 8 * rows * width,
            transcendentals=rows * keys * (width // HEAD_DIM),
        ),
        name="attn_fwd",
    )(q, k, v, bias)


def attn_bwd_kernel(q_ref, g_ref, k_ref, v_ref, bias_ref, lse_ref, gq_ref, gk_ref, gv_ref, gk_acc, gv_acc):
    step = pl.program_id(0)
    rows, width = q_ref.shape
    heads = width // HEAD_DIM
    lane = lax.broadcasted_iota(jnp.int32, (1, width), 1) // HEAD_DIM
    q = q_ref[...]
    g = g_ref[...]
    k = k_ref[...]
    v = v_ref[...]
    bias = bias_ref[...]
    lse = lse_ref[...]
    gq = jnp.zeros((rows, width), f32)

    @pl.when(step == 0)
    def _():
        gk_acc[...] = jnp.zeros_like(gk_acc)
        gv_acc[...] = jnp.zeros_like(gv_acc)

    for h in range(heads):
        mine = lane == h
        qh = jnp.where(mine, q, jnp.zeros_like(q))
        gh = jnp.where(mine, g, jnp.zeros_like(g))
        s = dot_nt(qh, k) * SCORE_SCALE + bias
        p = jnp.exp2(s - lse[:, h : h + 1])
        dp = dot_nt(gh, v)
        inner = jnp.sum(p * dp, axis=1, keepdims=True)
        ds = (p * (dp - inner)).astype(bf16)
        p_low = p.astype(bf16)
        gq = jnp.where(mine, dot_nn(ds, k), gq)
        gk_acc[...] += dot_tn(ds, qh)
        gv_acc[...] += dot_tn(p_low, gh)
    gq_ref[...] = (gq * 0.125).astype(bf16)

    @pl.when(step == pl.num_programs(0) - 1)
    def _():
        gk_ref[...] = (gk_acc[...] * 0.125).astype(bf16)
        gv_ref[...] = gv_acc[...].astype(bf16)


def attn_bwd(q, g, k, v, bias, lse, block):
    rows, width = q.shape
    keys = k.shape[0]
    full = pl.BlockSpec((keys, width), lambda i: (0, 0))
    part = pl.BlockSpec((block, width), lambda i: (i, 0))
    return pl.pallas_call(
        attn_bwd_kernel,
        grid=(rows // block,),
        in_specs=[
            part,
            part,
            full,
            full,
            pl.BlockSpec((1, keys), lambda i: (0, 0)),
            pl.BlockSpec((block, 128), lambda i: (i, 0)),
        ],
        out_specs=[part, full, full],
        out_shape=[
            jax.ShapeDtypeStruct((rows, width), bf16),
            jax.ShapeDtypeStruct((keys, width), bf16),
            jax.ShapeDtypeStruct((keys, width), bf16),
        ],
        scratch_shapes=[pltpu.VMEM((keys, width), f32), pltpu.VMEM((keys, width), f32)],
        compiler_params=pltpu.CompilerParams(vmem_limit_bytes=VMEM_LIMIT),
        cost_estimate=pl.CostEstimate(
            flops=10 * rows * keys * width * (width // HEAD_DIM),
            bytes_accessed=12 * keys * width,
            transcendentals=rows * keys * (width // HEAD_DIM),
        ),
        name="attn_bwd",
    )(q, g, k, v, bias, lse)


def swap_core(value):
    return lax.ppermute(value, "mp", [(i, i ^ 1) for i in range(4)])


def swap_chip(value):
    return lax.ppermute(value, "mp", [(i, i ^ 2) for i in range(4)])


def gather_rows(own):
    other = swap_chip(own)
    sibling = swap_core(own)
    diagonal = swap_core(other)
    return own, sibling, other, diagonal


def scatter_rows(part):
    from_sibling = swap_core(part(3))
    from_chip = swap_chip(part(2) + from_sibling)
    near = swap_core(part(1))
    return part(0) + near + from_chip


def rounder(count):
    one = jnp.minimum(count, 1).astype(f32)
    return lambda value: (value * one).astype(bf16)


def bit_order_blocks(parts, order):
    bits = len(order)
    blocks = []
    for position in range(parts):
        block = 0
        for level, bit in enumerate(order):
            block |= ((position >> (bits - 1 - level)) & 1) << bit
        blocks.append(block)
    return blocks


def bit_order_columns(matrix, parts, order):
    width = matrix.shape[1] // parts
    return jnp.concatenate(
        [matrix[:, b * width : (b + 1) * width] for b in bit_order_blocks(parts, order)], axis=1
    )


def halving_sum(left, right, parts, order, place):
    def swap(value, bit):
        return lax.ppermute(value, "dp", [(i, i ^ (1 << bit)) for i in range(parts)])

    if not order:
        return dot_tn(left, right)
    half = left.shape[1] // 2
    mine = (place >> order[0]) & 1
    away = dot_tn(lax.dynamic_slice_in_dim(left, (1 - mine) * half, half, 1), right)
    got = swap(away, order[0])
    total = dot_tn(lax.dynamic_slice_in_dim(left, mine * half, half, 1), right) + got
    for bit in order[1:]:
        half = total.shape[0] // 2
        mine = (place >> bit) & 1
        away = lax.dynamic_slice_in_dim(total, (1 - mine) * half, half, 0)
        got = swap(away, bit)
        total = lax.dynamic_slice_in_dim(total, mine * half, half, 0) + got
    return total


def sum_over(value, axis, parts):
    step = 1
    while step < parts:
        value = value + lax.ppermute(value, axis, [(i, i ^ step) for i in range(parts)])
        step *= 2
    return value


def row_norm(values):
    centre = values - jnp.mean(values, axis=-1, keepdims=True)
    spread = jnp.mean(centre * centre, axis=-1, keepdims=True)
    scale_inv = lax.rsqrt(spread + NORM_EPS)
    return centre * scale_inv, scale_inv


def norm_back(grad_rows, unit_rows, scale_inv, gain):
    scaled = grad_rows * gain
    return scale_inv * (
        scaled
        - jnp.mean(scaled, axis=-1, keepdims=True)
        - unit_rows * jnp.mean(scaled * unit_rows, axis=-1, keepdims=True)
    )


def col_sum(rows):
    return jnp.sum(rows, axis=0)


def shards(
    dp_size,
    tokens,
    doc_lengths,
    cls_pos,
    cls_count,
    q_weight,
    q_bias,
    k_weight,
    v_weight,
    v_bias,
    o_weight,
    o_bias,
    ln1_gain,
    ln1_bias,
    up_weight,
    up_bias,
    down_weight,
    down_bias,
    ln2_gain,
    ln2_bias,
    out_grad,
    pooled_grad,
):
    slot_len, width = tokens.shape
    rows = slot_len // 4
    rank = lax.axis_index("mp")
    place = lax.axis_index("dp")
    bits = dp_size.bit_length() - 1
    order_a = list(range(bits))
    order_b = [1, 0] + list(range(2, bits)) if bits > 1 else order_a
    length = doc_lengths[0]
    rounded = rounder(cls_count[0])
    blocks = [rank ^ j for j in range(4)]

    def take(array, j):
        return lax.dynamic_slice_in_dim(array, blocks[j] * rows, rows, 0)

    o_near = o_weight
    o_far = rounded(swap_chip(o_weight.astype(f32)))
    gain_one = ln1_gain.astype(f32)
    gain_two = ln2_gain.astype(f32)
    shift_one = ln1_bias.astype(f32)
    shift_two = ln2_bias.astype(f32)

    local = jnp.concatenate([take(tokens, j) for j in range(4)], axis=0)
    row_ids = lax.iota(jnp.int32, rows)
    positions = jnp.concatenate([row_ids + blocks[j] * rows for j in range(4)])
    bias = jnp.where(positions < length, 0.0, MASKED).astype(f32)[None, :]
    queries = (dot_nn(local, q_weight) + q_bias.astype(f32)).astype(bf16)
    key_rows = dot_nn(local, k_weight).astype(bf16)
    value_rows = (dot_nn(local, v_weight) + v_bias.astype(f32)).astype(bf16)

    half = 2 * rows
    away_context, lse_far = attn_fwd(queries[half:], key_rows, value_rows, bias, 256, f32)
    context_far = away_context.astype(bf16)
    context_other = rounded(swap_chip(away_context))
    context_near, lse_near = attn_fwd(queries[:half], key_rows, value_rows, bias, 256, bf16)

    def attended_part(j):
        cut = slice(j * rows, (j + 1) * rows)
        return dot_nn(context_near[cut], o_near) + dot_nn(context_other[cut], o_far)

    attended = attended_part(0) + swap_core(attended_part(1)) + o_bias.astype(f32)
    unit_one, inv_one = row_norm(local[:rows].astype(f32) + attended)
    normed = unit_one * gain_one + shift_one
    n0, n1, n2, n3 = gather_rows(normed)
    low_near = jnp.concatenate([n0.astype(bf16), rounded(n1)], axis=0)
    low_far = jnp.concatenate([rounded(n2), rounded(n3)], axis=0)

    def feed(low):
        pre = dot_nn(low, up_weight) + up_bias.astype(f32)
        return pre, jax.nn.gelu(pre, approximate=False).astype(bf16)

    pre_near, active_near = feed(low_near)
    pre_far, active_far = feed(low_far)

    def pick(near, far, j):
        source = near if j < 2 else far
        return source[(j % 2) * rows : (j % 2 + 1) * rows]

    fed = scatter_rows(lambda j: dot_nn(pick(active_near, active_far, j), down_weight))
    second = gather_rows(normed + fed + down_bias.astype(f32))

    outs = []
    grads_low = []
    markers = []
    for j in range(4):
        unit_two, inv_two = row_norm(second[j])
        keep = ((row_ids + blocks[j] * rows) < length).astype(f32)[:, None]
        outs.append(((unit_two * gain_two + shift_two) * keep).astype(bf16))
        spot = lax.dynamic_index_in_dim(cls_pos[0], blocks[j], keepdims=False) - blocks[j] * rows
        live = blocks[j] < cls_count[0]
        extra = lax.dynamic_index_in_dim(pooled_grad[0], blocks[j], keepdims=True)
        placed = jnp.where(((row_ids == spot) & live)[:, None], extra, 0.0)
        grad_out = (take(out_grad, j).astype(f32) + placed) * keep
        grad_two = norm_back(grad_out, unit_two, inv_two, gain_two)
        grads_low.append(grad_two.astype(bf16))
        marker = lax.dynamic_slice_in_dim(second[j], jnp.clip(spot, 0, rows - 1), 1, 0)
        markers.append(marker)
        if j == 0:
            grad_two_own = grad_two
            ln2_gain_grad = col_sum(grad_out * unit_two)
            ln2_bias_grad = col_sum(grad_out)
            down_bias_grad = col_sum(grads_low[0].astype(f32))
    marked = jnp.concatenate(
        [
            lax.dynamic_index_in_dim(
                jnp.concatenate(markers, axis=0), rank ^ j, keepdims=True
            )
            for j in range(4)
        ],
        axis=0,
    )
    marked_unit, _ = row_norm(marked)
    valid = (lax.iota(jnp.int32, 4) < cls_count[0]).astype(f32)[:, None]
    pooled = ((marked_unit * gain_two + shift_two) * valid)[None]

    grad_near = jnp.concatenate(grads_low[:2], axis=0)
    grad_far = jnp.concatenate(grads_low[2:], axis=0)

    def slope(pre):
        normal_cdf = 0.5 * (1.0 + lax.erf(pre * ROOT_HALF))
        density = jnp.exp(-0.5 * pre * pre) * INV_ROOT_TAU
        return normal_cdf + pre * density

    grad_pre_near = (dot_nt(grad_near, down_weight) * slope(pre_near)).astype(bf16)
    grad_pre_far = (dot_nt(grad_far, down_weight) * slope(pre_far)).astype(bf16)
    up_bias_grad = col_sum(grad_pre_near.astype(f32)) + col_sum(grad_pre_far.astype(f32))
    back = scatter_rows(lambda j: dot_nt(pick(grad_pre_near, grad_pre_far, j), up_weight))

    active = jnp.concatenate([active_near, active_far], axis=0)
    grad_fed = jnp.concatenate([grad_near, grad_far], axis=0)
    normed_low = jnp.concatenate([low_near, low_far], axis=0)
    grad_pre = jnp.concatenate([grad_pre_near, grad_pre_far], axis=0)
    down_sum = halving_sum(
        bit_order_columns(grad_fed, dp_size, order_a), active, dp_size, order_a, place
    ).T
    up_sum = halving_sum(
        bit_order_columns(normed_low, dp_size, order_b), grad_pre, dp_size, order_b, place
    )

    grad_normed = grad_two_own + back
    grad_first = norm_back(grad_normed, unit_one, inv_one, gain_one)
    ln1_gain_grad = col_sum(grad_normed * unit_one)
    ln1_bias_grad = col_sum(grad_normed)
    grad_attended_own = grad_first.astype(bf16)
    o_bias_grad = col_sum(grad_attended_own.astype(f32))
    grad_attended = jnp.concatenate(
        [grad_attended_own, rounded(swap_core(grad_first))], axis=0
    )
    grad_context_far = rounded(swap_chip(dot_nt(grad_attended, o_far)))
    grad_context_near = dot_nt(grad_attended, o_near).astype(bf16)
    grad_context = jnp.concatenate([grad_context_near, grad_context_far], axis=0)

    ga_cols = bit_order_columns(grad_attended, dp_size, order_b)
    o_part = dot_tn(ga_cols, context_near) + swap_chip(dot_tn(ga_cols, context_other))

    grad_q, grad_k, grad_v = attn_bwd(
        queries,
        grad_context,
        key_rows,
        value_rows,
        bias,
        jnp.concatenate([lse_near, lse_far], axis=0),
        256,
    )
    grad_qkv = jnp.concatenate([grad_q, grad_k, grad_v], axis=1)
    qkv_weight = jnp.concatenate([q_weight, k_weight, v_weight], axis=1)
    in_own = grad_first + scatter_rows(
        lambda j: dot_nt(grad_qkv[j * rows : (j + 1) * rows], qkv_weight)
    )
    in_parts = gather_rows(in_own)

    def place_rows(parts):
        result = jnp.zeros((slot_len, width), parts[0].dtype)
        for j in range(4):
            result = lax.dynamic_update_slice_in_dim(result, parts[j], blocks[j] * rows, 0)
        return result

    qkv_sum = halving_sum(
        bit_order_columns(local, dp_size, order_a), grad_qkv, dp_size, order_a, place
    )

    def rest(total, order):
        for bit in order:
            cut = total.shape[0] // 2
            mine = (place >> bit) & 1
            away = lax.dynamic_slice_in_dim(total, (1 - mine) * cut, cut, 0)
            got = lax.ppermute(away, "dp", [(i, i ^ (1 << bit)) for i in range(dp_size)])
            total = lax.dynamic_slice_in_dim(total, mine * cut, cut, 0) + got
        return total

    o_sum = rest(o_part, order_b).T
    head_width = q_weight.shape[1]
    q_bias_grad = col_sum(grad_q.astype(f32))
    v_bias_grad = col_sum(grad_v.astype(f32))
    shared = sum_over(
        jnp.stack(
            [o_bias_grad, ln1_gain_grad, ln1_bias_grad, down_bias_grad, ln2_gain_grad, ln2_bias_grad]
        ),
        "mp",
        4,
    )
    head_row = jnp.concatenate(
        [q_bias_grad, v_bias_grad, jnp.zeros((width - 2 * head_width,), f32)]
    )
    sums = sum_over(
        jnp.concatenate([shared, head_row[None], up_bias_grad[None]], axis=0), "dp", dp_size
    )
    q_sum = qkv_sum[:, :head_width]
    k_sum = qkv_sum[:, head_width : 2 * head_width]
    v_sum = qkv_sum[:, 2 * head_width :]
    return (
        place_rows(outs),
        pooled,
        place_rows(in_parts),
        q_sum,
        sums[6, :head_width],
        k_sum,
        v_sum,
        sums[6, head_width : 2 * head_width],
        o_sum,
        sums[0],
        sums[1],
        sums[2],
        up_sum,
        sums[7],
        down_sum,
        sums[3],
        sums[4],
        sums[5],
    )


def solution(mesh):
    return jax.shard_map(
        functools.partial(shards, mesh.shape["dp"]),
        mesh=mesh,
        in_specs=(
            P("dp", None),
            P("dp"),
            P("dp", None),
            P("dp"),
            P(None, "mp"),
            P("mp"),
            P(None, "mp"),
            P(None, "mp"),
            P("mp"),
            P("mp", None),
            P(),
            P(),
            P(),
            P(None, "mp"),
            P("mp"),
            P("mp", None),
            P(),
            P(),
            P(),
            P("dp", None),
            P("dp", None, None),
        ),
        out_specs=(
            P("dp", None),
            P("dp", None, None),
            P("dp", None),
            P("dp", "mp"),
            P("mp"),
            P("dp", "mp"),
            P("dp", "mp"),
            P("mp"),
            P("mp", "dp"),
            P(),
            P(),
            P(),
            P("dp", "mp"),
            P("mp"),
            P("mp", "dp"),
            P(),
            P(),
            P(),
        ),
        check_vma=False,
    )
```

time: 943 us -> 402 us (0.43)
  waiting for transfers between devices: 704 us -> 162 us
  matrix products: 104 us -> 59 us
  starting transfers between devices: 1.38 us -> 41.9 us
  blocking collectives: 37.8 us -> 0 us
  Pallas kernels: 0 us -> 27.4 us
  local copies, waits for them, and re-layouts: 25 us -> 44.3 us
  other arithmetic: 41.3 us -> 55.9 us
  between operations: 16.3 us -> 6.7 us
    reduce_scatter x6 -> x0, waiting for transfers between devices: 362 us -> none  [the longest x1 92.2 us: shards(): lax.psum_scatter(ffn_pair[0], 'dp', scatter_dimension=0, tiled=True)]
    psum x4 -> x0, waiting for transfers between devices: 342 us -> none  [the longest x1 87.6 us: shards(): lax.psum(jnp.dot(context_low, o_weight, preferred_element_type=jnp.float3...]
    ppermute x0 -> x41, waiting for transfers between devices: none -> 162 us  [the longest x10 94.5 us: swap_chip(): return lax.ppermute(value, 'mp', [(i, i ^ 2) for i in range(4)])]
    dot_general x34 -> x33, matrix products: 104 us -> 59 us  [the longest x13 25.2 us: dot_nn(): lax.dot_general(a, b, (((1,), (0,)), ((), ())), preferred_element_type=f32)]
    ppermute x0 -> x41, starting transfers between devices: none -> 41.9 us  [the longest x9 17 us: swap(): return lax.ppermute(value, 'dp', [(i, i ^ 1 << bit) for i in range(parts)])]
    psum x1 -> x0, blocking collectives: 37.8 us -> none  [shards(): lax.psum((q_bias_grad, v_bias_grad, o_bias_grad, ln1_gain_grad, ln1_bias_...]
    pallas_call x0 -> x3, Pallas kernels: none -> 27.4 us  [the longest x1 17.6 us: attn_bwd(): pl.pallas_call(attn_bwd_kernel, grid=(rows // block,), in_specs=[part, pa...]
    convert_element_type x13 -> x25, other arithmetic: 6.11 us -> 18.3 us  [the longest x7 7.77 us: rounder(): return lambda value: (value * one).astype(bf16)]
  transfers between devices with their start and end apart: 10 -> 41, of which waited for: 9 -> 17; matrix products, arithmetic and copies ran while one was open for 5% -> 26% of each run, Pallas kernels for 0% -> 7%
where the time goes in v1:
time: 402 us; the launch traced here: 398 us
  waiting for transfers between devices  162 us (40%)
  matrix products  59 us (15%)
  other arithmetic  55.9 us (14%)
  local copies, waits for them, and re-layouts  44.3 us (11%)
  starting transfers between devices  41.9 us (10%)
  Pallas kernels  27.4 us (7%)
  between operations  6.7 us (2%)
    ppermute x10, waiting for transfers between devices, swap_chip(): return lax.ppermute(value, 'mp', [(i, i ^ 2) for i in range(4)])  94.5 us
    ppermute x9, waiting for transfers between devices, swap(): return lax.ppermute(value, 'dp', [(i, i ^ 1 << bit) for i in range(parts)])  45 us
    dot_general x13, matrix products, dot_nn(): lax.dot_general(a, b, (((1,), (0,)), ((), ())), preferred_element_type=f32)  25.2 us
    unnamed x163, local copies, waits for them, and re-layouts  20.8 us
    ppermute x3, waiting for transfers between devices, rest(): got = lax.ppermute(away, 'dp', [(i, i ^ 1 << bit) for i in range(dp_size)])  19.5 us
    dot_general x12, matrix products, dot_nt(): lax.dot_general(a, b, (((1,), (1,)), ((), ())), preferred_element_type=f32)  18.5 us
    pallas_call x1, Pallas kernels, attn_bwd(): pl.pallas_call(attn_bwd_kernel, grid=(rows // block,), in_specs=[part, pa...  17.6 us
    ppermute x9, starting transfers between devices, swap(): return lax.ppermute(value, 'dp', [(i, i ^ 1 << bit) for i in range(parts)])  17 us
  transfers between devices with their start and end apart: 41, of which 17 were waited for; matrix products, arithmetic and copies ran while one was open for 26% of the time, Pallas kernels for 7%

profile of v1, /device:TPU:0, one launch (start us, length us, event | category | flops | bytes accessed | tf_op | source)
XLA Modules:
  0.0 397.7 jit_solution(1100621145798825215)
XLA Ops:
  2.9 2.9 collective-permute-start.1
  14.5 5.4 %attn_fwd.3 = (f32[512,256]{1,0:T(8,128)}, f32[512,128]{1,0:T(8,128)S(1)}) custom-call(bf16[512,256]{1,0:T(8,128)(2,1)S(1)} %get-tuple-element.79.q_ref, bf16[1024,256]{1,0:T(8,128)(2,1)S(1)} %convolution_convert_fusion.k_ref, bf16[1024,256]{1,0:T(8,128)(2,1)S(1)} %fusion.45.v_ref, f32[1,1024]{1,0:T(1,128)S(1)} %compare_select_fusion.bias_ref), custom_call_target="tpu_custom_call" | custom-call | flops 2147483648 | bytes 2097152 | tf_op jit(solution)/shard_map/attn_fwd/pallas_call | solution.py:64
  29.1 4.4 %attn_fwd.2 = (bf16[512,256]{1,0:T(8,128)(2,1)S(1)}, f32[512,128]{1,0:T(8,128)S(1)}) custom-call(bf16[512,256]{1,0:T(8,128)(2,1)S(1)} %copy-done.2, bf16[1024,256]{1,0:T(8,128)(2,1)S(1)} %copy-done.5, bf16[1024,256]{1,0:T(8,128)(2,1)S(1)} %copy-done.8, f32[1,1024]{1,0:T(1,128)S(1)} %compare_select_fusion.bias_ref), custom_call_target="tpu_custom_call" | custom-call | flops 2147483648 | bytes 2097152 | tf_op jit(solution)/shard_map/attn_fwd/pallas_call | solution.py:64
  33.9 6.7 %collective-permute-done = f32[512,256]{1,0:T(8,128)} collective-permute-done((f32[512,256]{1,0:T(8,128)}, f32[512,256]{1,0:T(8,128)}, u32[]{:S(2)}, u32[]{:S(2)}) %collective-permute-start) | collective-permute-done | bytes 524320 | tf_op jit(solution)/shard_map/ppermute | solution.py:168
  57.5 21.9 %collective-permute-done.5 = f32[256,1024]{1,0:T(8,128)} collective-permute-done((f32[256,1024]{1,0:T(8,128)}, f32[256,1024]{1,0:T(8,128)}, u32[]{:S(2)}, u32[]{:S(2)}) %collective-permute-start.5) | collective-permute-done | bytes 1048608 | tf_op jit(solution)/shard_map/ppermute | solution.py:168
  89.0 12.0 %fusion.2 = (bf16[512,1024]{1,0:T(8,128)(2,1)S(1)}, bf16[512,1024]{1,0:T(8,128)(2,1)S(1)}, f32[512,1024]{1,0:T(8,128)}) fusion(f32[1024]{0:T(1024)S(1)} %convert_element_type.192, f32[512,1024]{1,0:T(8,128)S(1)} %fusion.50, bf16[1024,1024]{1,0:T(8,128)(2,1)S(1)} %copy-done, bf16[256,1024]{1,0:T(8,128)(2,1)S(1)} %multiply_convert_fusion.10, ...), kind=kOutput, calls=%fused_computation.23 | convolution fusion | flops 1145044992 | bytes 9441280 | tf_op jit(solution)/shard_map/dot_general | solution.py:24
  107.7 23.0 %collective-permute-done.8 = f32[256,1024]{1,0:T(8,128)S(1)} collective-permute-done((f32[256,1024]{1,0:T(8,128)S(1)}, f32[256,1024]{1,0:T(8,128)S(1)}, u32[]{:S(2)}, u32[]{:S(2)}) %collective-permute-start.8) | collective-permute-done | bytes 1048608 | tf_op jit(solution)/shard_map/ppermute | solution.py:168
  130.8 3.0 fusion.147
  142.0 16.8 %collective-permute-done.10 = f32[256,1024]{1,0:T(8,128)} collective-permute-done((f32[256,1024]{1,0:T(8,128)}, f32[256,1024]{1,0:T(8,128)}, u32[]{:S(2)}, u32[]{:S(2)}) %collective-permute-start.10) | collective-permute-done | bytes 1048608 | tf_op jit(solution)/shard_map/ppermute | solution.py:168
  163.1 3.0 multiply_reduce_fusion
  170.1 2.7 convert_reduce_fusion.1
  185.8 2.9 fusion.68
  192.4 2.9 convert_reduce_fusion
  197.9 2.7 fusion.42
  202.3 2.7 fusion.43
  212.3 20.4 %collective-permute-done.14 = f32[256,1024]{1,0:T(8,128)S(1)} collective-permute-done((f32[256,1024]{1,0:T(8,128)S(1)}, f32[256,1024]{1,0:T(8,128)S(1)}, u32[]{:S(2)}, u32[]{:S(2)}) %collective-permute-start.14) | collective-permute-done | bytes 1048608 | tf_op jit(solution)/shard_map/ppermute | solution.py:168
  232.8 3.8 multiply_reduce_fusion.1
  239.5 9.0 %collective-permute-done.38 = f32[512,1024]{1,0:T(8,128)} collective-permute-done((f32[512,1024]{1,0:T(8,128)}, f32[512,1024]{1,0:T(8,128)}, u32[]{:S(2)}, u32[]{:S(2)}) %collective-permute-start.38) | collective-permute-done | bytes 2097184 | tf_op jit(solution)/shard_map/ppermute | solution.py:210
  248.5 4.0 convolution_add_fusion
  254.5 2.9 convolution_add_fusion.1
  267.5 9.5 %collective-permute-done.39 = f32[256,1024]{1,0:T(8,128)S(1)} collective-permute-done((f32[256,1024]{1,0:T(8,128)S(1)}, f32[256,1024]{1,0:T(8,128)S(1)}, u32[]{:S(2)}, u32[]{:S(2)}) %collective-permute-start.39) | collective-permute-done | bytes 1048608 | tf_op jit(solution)/shard_map/ppermute | solution.py:210
  277.3 2.8 collective-permute-start.40
  280.1 2.8 collective-permute-done.36
  284.3 17.6 %attn_bwd.1 = (bf16[1024,256]{1,0:T(8,128)(2,1)S(1)}, bf16[1024,256]{1,0:T(8,128)(2,1)S(1)}, bf16[1024,256]{1,0:T(8,128)(2,1)S(1)}) custom-call(bf16[1024,256]{1,0:T(8,128)(2,1)S(1)} %fusion.44.q_ref, bf16[1024,256]{1,0:T(8,128)(2,1)S(1)} %pad_maximum_fusion.12.g_ref, bf16[1024,256]{1,0:T(8,128)(2,1)S(1)} %copy-done.6, bf16[1024,256]{1,0:T(8,128)(2,1)S(1)} %copy-done.9, ...), custom_call_target="tpu_custom_call" | custom-call | flops 10737418240 | bytes 3145728 | tf_op jit(solution)/shard_map/attn_bwd/pallas_call | solution.py:135
  314.5 2.6 collective-permute-start.37
  317.1 19.5 %collective-permute-done.32 = f32[512,256]{1,0:T(8,128)S(1)} collective-permute-done((f32[512,256]{1,0:T(8,128)S(1)}, f32[512,256]{1,0:T(8,128)S(1)}, u32[]{:S(2)}, u32[]{:S(2)}) %collective-permute-start.32) | collective-permute-done | bytes 524320 | tf_op jit(solution)/shard_map/ppermute | solution.py:445
  336.7 7.5 %collective-permute-done.23 = f32[512,768]{1,0:T(8,128)S(1)} collective-permute-done((f32[512,768]{1,0:T(8,128)S(1)}, f32[512,768]{1,0:T(8,128)S(1)}, u32[]{:S(2)}, u32[]{:S(2)}) %collective-permute-start.23) | collective-permute-done | bytes 1572896 | tf_op jit(solution)/shard_map/ppermute | solution.py:210
  350.0 2.9 constant_dynamic-update-slice_fusion.9
  359.0 2.7 collective-permute-start.34
  361.7 6.9 %collective-permute-done.24 = f32[256,768]{1,0:T(8,128)} collective-permute-done((f32[256,768]{1,0:T(8,128)}, f32[256,768]{1,0:T(8,128)}, u32[]{:S(2)}, u32[]{:S(2)}) %collective-permute-start.24) | collective-permute-done | bytes 786464 | tf_op jit(solution)/shard_map/ppermute | solution.py:210
  372.6 5.6 %collective-permute-done.21 = f32[256,1024]{1,0:T(8,128)} collective-permute-done((f32[256,1024]{1,0:T(8,128)}, f32[256,1024]{1,0:T(8,128)}, u32[]{:S(2)}, u32[]{:S(2)}) %collective-permute-start.21) | collective-permute-done | bytes 1048608 | tf_op jit(solution)/shard_map/ppermute | solution.py:168
  379.6 9.2 %collective-permute-done.25 = f32[128,768]{1,0:T(8,128)} collective-permute-done((f32[128,768]{1,0:T(8,128)}, f32[128,768]{1,0:T(8,128)}, u32[]{:S(2)}, u32[]{:S(2)}) %collective-permute-start.25) | collective-permute-done | bytes 393248 | tf_op jit(solution)/shard_map/ppermute | solution.py:210
  (387 shorter events, 148.0 us)
Async XLA Ops:
  2.9 38.8 %collective-permute-start.1 = (f32[256,1024]{1,0:T(8,128)}, f32[256,1024]{1,0:T(8,128)}, u32[]{:S(2)}, u32[]{:S(2)}) collective-permute-start(f32[256,1024]{1,0:T(8,128)} %convert_element_type.185), channel_id=1, source_target_pairs={{0,2},{1,3},{2,0},{3,1},{4,6},{5,7},{6,4},{7,5},{8,10},{9,11},{10,... | collective-permute-start | bytes 3145736 | tf_op jit(solution)/shard_map/ppermute | solution.py:168
  20.6 20.0 %collective-permute-start = (f32[512,256]{1,0:T(8,128)}, f32[512,256]{1,0:T(8,128)}, u32[]{:S(2)}, u32[]{:S(2)}) collective-permute-start(f32[512,256]{1,0:T(8,128)} %get-tuple-element.26), channel_id=1, source_target_pairs={{0,2},{1,3},{2,0},{3,1},{4,6},{5,7},{6,4},{7,5},{8,10},{9,11},{10,... | collective-permute-start | bytes 1572872 | tf_op jit(solution)/shard_map/ppermute | solution.py:168
  53.6 25.9 %collective-permute-start.5 = (f32[256,1024]{1,0:T(8,128)}, f32[256,1024]{1,0:T(8,128)}, u32[]{:S(2)}, u32[]{:S(2)}) collective-permute-start(f32[256,1024]{1,0:T(8,128)} %get-tuple-element.74), channel_id=1, source_target_pairs={{0,2},{1,3},{2,0},{3,1},{4,6},{5,7},{6,4},{7,5},{8,10},{9,11},{10,... | collective-permute-start | bytes 3145736 | tf_op jit(solution)/shard_map/ppermute | solution.py:168
  55.7 29.3 %collective-permute-start.3 = (f32[256,1024]{1,0:T(8,128)}, f32[256,1024]{1,0:T(8,128)}, u32[]{:S(2)}, u32[]{:S(2)}) collective-permute-start(f32[256,1024]{1,0:T(8,128)} %get-tuple-element.74), channel_id=1, source_target_pairs={{0,1},{1,0},{2,3},{3,2},{4,5},{5,4},{6,7},{7,6},{8,9},{9,8},{10,11... | collective-permute-start | bytes 3145736 | tf_op jit(solution)/shard_map/ppermute | solution.py:164
  105.3 25.5 %collective-permute-start.8 = (f32[256,1024]{1,0:T(8,128)S(1)}, f32[256,1024]{1,0:T(8,128)S(1)}, u32[]{:S(2)}, u32[]{:S(2)}) collective-permute-start(f32[256,1024]{1,0:T(8,128)S(1)} %convolution_add_fusion.9), channel_id=1, source_target_pairs={{0,2},{1,3},{2,0},{3,1},{4,6},{5,7},{6,4},{7,5},{8,10},{9,11},{10,... | collective-permute-start | bytes 3145736 | tf_op jit(solution)/shard_map/ppermute | solution.py:168
  133.8 24.9 %collective-permute-start.10 = (f32[256,1024]{1,0:T(8,128)}, f32[256,1024]{1,0:T(8,128)}, u32[]{:S(2)}, u32[]{:S(2)}) collective-permute-start(f32[256,1024]{1,0:T(8,128)} %get-tuple-element.111), channel_id=1, source_target_pairs={{0,2},{1,3},{2,0},{3,1},{4,6},{5,7},{6,4},{7,5},{8,10},{9,11},{10,... | collective-permute-start | bytes 3145736 | tf_op jit(solution)/shard_map/ppermute | solution.py:168
  135.7 24.4 %collective-permute-start.9 = (f32[256,1024]{1,0:T(8,128)}, f32[256,1024]{1,0:T(8,128)}, u32[]{:S(2)}, u32[]{:S(2)}) collective-permute-start(f32[256,1024]{1,0:T(8,128)} %get-tuple-element.111), channel_id=1, source_target_pairs={{0,1},{1,0},{2,3},{3,2},{4,5},{5,4},{6,7},{7,6},{8,9},{9,8},{10,11... | collective-permute-start | bytes 3145736 | tf_op jit(solution)/shard_map/ppermute | solution.py:164
  174.6 37.7 %collective-permute-start.12 = (f32[256,1024]{1,0:T(8,128)}, f32[256,1024]{1,0:T(8,128)}, u32[]{:S(2)}, u32[]{:S(2)}) collective-permute-start(f32[256,1024]{1,0:T(8,128)} %fusion.81), channel_id=1, source_target_pairs={{0,1},{1,0},{2,3},{3,2},{4,5},{5,4},{6,7},{7,6},{8,9},{9,8},{10,11... | collective-permute-start | bytes 3145736 | tf_op jit(solution)/shard_map/ppermute | solution.py:164
  196.3 10.9 %collective-permute-start.13 = (f32[256,1024]{1,0:T(8,128)S(1)}, f32[256,1024]{1,0:T(8,128)S(1)}, u32[]{:S(2)}, u32[]{:S(2)}) collective-permute-start(f32[256,1024]{1,0:T(8,128)S(1)} %fusion.78), channel_id=1, source_target_pairs={{0,1},{1,0},{2,3},{3,2},{4,5},{5,4},{6,7},{7,6},{8,9},{9,8},{10,11... | collective-permute-start | bytes 3145736 | tf_op jit(solution)/shard_map/ppermute | solution.py:164
  200.5 48.0 %collective-permute-start.38 = (f32[512,1024]{1,0:T(8,128)}, f32[512,1024]{1,0:T(8,128)}, u32[]{:S(2)}, u32[]{:S(2)}) collective-permute-start(f32[512,1024]{1,0:T(8,128)} %fusion.42), channel_id=1, source_target_pairs={{0,4},{4,0},{8,12},{12,8},{16,20},{20,16},{24,28},{28,24},{1,5},{5... | collective-permute-start | bytes 6291464 | tf_op jit(solution)/shard_map/ppermute | solution.py:210
  205.0 49.5 %collective-permute-start.35 = (f32[512,1024]{1,0:T(8,128)}, f32[512,1024]{1,0:T(8,128)}, u32[]{:S(2)}, u32[]{:S(2)}) collective-permute-start(f32[512,1024]{1,0:T(8,128)} %fusion.43), channel_id=1, source_target_pairs={{0,8},{4,12},{8,0},{12,4},{16,24},{20,28},{24,16},{28,20},{1,9},{5... | collective-permute-start | bytes 6291464 | tf_op jit(solution)/shard_map/ppermute | solution.py:210
  208.1 24.7 %collective-permute-start.14 = (f32[256,1024]{1,0:T(8,128)S(1)}, f32[256,1024]{1,0:T(8,128)S(1)}, u32[]{:S(2)}, u32[]{:S(2)}) collective-permute-start(f32[256,1024]{1,0:T(8,128)S(1)} %convolution_add_fusion.7), channel_id=1, source_target_pairs={{0,2},{1,3},{2,0},{3,1},{4,6},{5,7},{6,4},{7,5},{8,10},{9,11},{10,... | collective-permute-start | bytes 3145736 | tf_op jit(solution)/shard_map/ppermute | solution.py:168
  238.2 23.2 %collective-permute-start.15 = (f32[256,1024]{1,0:T(8,128)}, f32[256,1024]{1,0:T(8,128)}, u32[]{:S(2)}, u32[]{:S(2)}) collective-permute-start(f32[256,1024]{1,0:T(8,128)} %get-tuple-element.72), channel_id=1, source_target_pairs={{0,1},{1,0},{2,3},{3,2},{4,5},{5,4},{6,7},{7,6},{8,9},{9,8},{10,11... | collective-permute-start | bytes 3145736 | tf_op jit(solution)/shard_map/ppermute | solution.py:164
  238.9 18.5 %collective-permute-start.26 = (f32[6,1024]{1,0:T(8,128)S(1)}, f32[6,1024]{1,0:T(8,128)S(1)}, u32[]{:S(2)}, u32[]{:S(2)}) collective-permute-start(f32[6,1024]{1,0:T(8,128)S(1)} %stack.27), channel_id=1, source_target_pairs={{0,1},{1,0},{2,3},{3,2},{4,5},{5,4},{6,7},{7,6},{8,9},{9,8},{10,11... | collective-permute-start | bytes 73736 | tf_op jit(solution)/shard_map/ppermute | solution.py:231
  252.6 24.4 %collective-permute-start.39 = (f32[256,1024]{1,0:T(8,128)S(1)}, f32[256,1024]{1,0:T(8,128)S(1)}, u32[]{:S(2)}, u32[]{:S(2)}) collective-permute-start(f32[256,1024]{1,0:T(8,128)S(1)} %constant_dynamic-slice_fusion.1), channel_id=1, source_target_pairs={{0,8},{4,12},{8,0},{12,4},{16,24},{20,28},{24,16},{28,20},{1,9},{5... | collective-permute-start | bytes 3145736 | tf_op jit(solution)/shard_map/ppermute | solution.py:210
  259.1 23.8 %collective-permute-start.36 = (f32[256,1024]{1,0:T(8,128)S(1)}, f32[256,1024]{1,0:T(8,128)S(1)}, u32[]{:S(2)}, u32[]{:S(2)}) collective-permute-start(f32[256,1024]{1,0:T(8,128)S(1)} %constant_dynamic-slice_fusion.3), channel_id=1, source_target_pairs={{0,4},{4,0},{8,12},{12,8},{16,20},{20,16},{24,28},{28,24},{1,5},{5... | collective-permute-start | bytes 3145736 | tf_op jit(solution)/shard_map/ppermute | solution.py:210
  263.3 19.9 %collective-permute-start.16 = (f32[512,256]{1,0:T(8,128)S(1)}, f32[512,256]{1,0:T(8,128)S(1)}, u32[]{:S(2)}, u32[]{:S(2)}) collective-permute-start(f32[512,256]{1,0:T(8,128)S(1)} %fusion.73), channel_id=1, source_target_pairs={{0,2},{1,3},{2,0},{3,1},{4,6},{5,7},{6,4},{7,5},{8,10},{9,11},{10,... | collective-permute-start | bytes 1572872 | tf_op jit(solution)/shard_map/ppermute | solution.py:168
  266.5 43.7 %collective-permute-start.31 = (f32[1024,256]{1,0:T(8,128)S(1)}, f32[1024,256]{1,0:T(8,128)S(1)}, u32[]{:S(2)}, u32[]{:S(2)}) collective-permute-start(f32[1024,256]{1,0:T(8,128)S(1)} %fusion.149), channel_id=1, source_target_pairs={{0,2},{1,3},{2,0},{3,1},{4,6},{5,7},{6,4},{7,5},{8,10},{9,11},{10,... | collective-permute-start | bytes 3145736 | tf_op jit(solution)/shard_map/ppermute | solution.py:168
  277.3 36.2 %collective-permute-start.40 = (f32[128,1024]{1,0:T(8,128)S(1)}, f32[128,1024]{1,0:T(8,128)S(1)}, u32[]{:S(2)}, u32[]{:S(2)}) collective-permute-start(f32[128,1024]{1,0:T(8,128)S(1)} %constant_dynamic-slice_fusion), channel_id=1, source_target_pairs={{0,16},{4,20},{8,24},{12,28},{16,0},{20,4},{24,8},{28,12},{1,17},{... | collective-permute-start | bytes 1572872 | tf_op jit(solution)/shard_map/ppermute | solution.py:210
  306.2 41.7 %collective-permute-start.17 = (f32[256,1024]{1,0:T(8,128)S(1)}, f32[256,1024]{1,0:T(8,128)S(1)}, u32[]{:S(2)}, u32[]{:S(2)}) collective-permute-start(f32[256,1024]{1,0:T(8,128)S(1)} %fusion.93), channel_id=1, source_target_pairs={{0,1},{1,0},{2,3},{3,2},{4,5},{5,4},{6,7},{7,6},{8,9},{9,8},{10,11... | collective-permute-start | bytes 3145736 | tf_op jit(solution)/shard_map/ppermute | solution.py:164
  308.7 35.6 %collective-permute-start.23 = (f32[512,768]{1,0:T(8,128)S(1)}, f32[512,768]{1,0:T(8,128)S(1)}, u32[]{:S(2)}, u32[]{:S(2)}) collective-permute-start(f32[512,768]{1,0:T(8,128)S(1)} %fusion.64), channel_id=1, source_target_pairs={{0,4},{4,0},{8,12},{12,8},{16,20},{20,16},{24,28},{28,24},{1,5},{5... | collective-permute-start | bytes 4718600 | tf_op jit(solution)/shard_map/ppermute | solution.py:210
  312.4 24.2 %collective-permute-start.32 = (f32[512,256]{1,0:T(8,128)S(1)}, f32[512,256]{1,0:T(8,128)S(1)}, u32[]{:S(2)}, u32[]{:S(2)}) collective-permute-start(f32[512,256]{1,0:T(8,128)S(1)} %constant_dynamic-slice_fusion.6), channel_id=1, source_target_pairs={{0,8},{4,12},{8,0},{12,4},{16,24},{20,28},{24,16},{28,20},{1,9},{5... | collective-permute-start | bytes 1572872 | tf_op jit(solution)/shard_map/ppermute | solution.py:445
  313.5 36.0 %collective-permute-start.19 = (f32[256,1024]{1,0:T(8,128)S(1)}, f32[256,1024]{1,0:T(8,128)S(1)}, u32[]{:S(2)}, u32[]{:S(2)}) collective-permute-start(f32[256,1024]{1,0:T(8,128)S(1)} %convolution_add_fusion.3), channel_id=1, source_target_pairs={{0,2},{1,3},{2,0},{3,1},{4,6},{5,7},{6,4},{7,5},{8,10},{9,11},{10,... | collective-permute-start | bytes 3145736 | tf_op jit(solution)/shard_map/ppermute | solution.py:168
  314.5 41.0 %collective-permute-start.37 = (f32[128,1024]{1,0:T(8,128)S(1)}, f32[128,1024]{1,0:T(8,128)S(1)}, u32[]{:S(2)}, u32[]{:S(2)}) collective-permute-start(f32[128,1024]{1,0:T(8,128)S(1)} %constant_dynamic-slice_fusion.2), channel_id=1, source_target_pairs={{0,16},{4,20},{8,24},{12,28},{16,0},{20,4},{24,8},{28,12},{1,17},{... | collective-permute-start | bytes 1572872 | tf_op jit(solution)/shard_map/ppermute | solution.py:210
  336.6 20.7 %collective-permute-start.30 = (f32[8,1024]{1,0:T(8,128)S(1)}, f32[8,1024]{1,0:T(8,128)S(1)}, u32[]{:S(2)}, u32[]{:S(2)}) collective-permute-start(f32[8,1024]{1,0:T(8,128)S(1)} %add.528), channel_id=1, source_target_pairs={{0,16},{4,20},{8,24},{12,28},{16,0},{20,4},{24,8},{28,12},{1,17},{... | collective-permute-start | bytes 98312 | tf_op jit(solution)/shard_map/ppermute | solution.py:231
  344.3 13.7 %collective-permute-start.33 = (f32[256,256]{1,0:T(8,128)S(1)}, f32[256,256]{1,0:T(8,128)}, u32[]{:S(2)}, u32[]{:S(2)}) collective-permute-start(f32[256,256]{1,0:T(8,128)S(1)} %constant_dynamic-slice_fusion.5), channel_id=1, source_target_pairs={{0,4},{4,0},{8,12},{12,8},{16,20},{20,16},{24,28},{28,24},{1,5},{5... | collective-permute-start | bytes 786440 | tf_op jit(solution)/shard_map/ppermute | solution.py:445
  347.9 20.7 %collective-permute-start.24 = (f32[256,768]{1,0:T(8,128)}, f32[256,768]{1,0:T(8,128)}, u32[]{:S(2)}, u32[]{:S(2)}) collective-permute-start(f32[256,768]{1,0:T(8,128)} %constant_dynamic-slice_fusion.8), channel_id=1, source_target_pairs={{0,8},{4,12},{8,0},{12,4},{16,24},{20,28},{24,16},{28,20},{1,9},{5... | collective-permute-start | bytes 2359304 | tf_op jit(solution)/shard_map/ppermute | solution.py:210
  355.0 23.2 %collective-permute-start.21 = (f32[256,1024]{1,0:T(8,128)}, f32[256,1024]{1,0:T(8,128)}, u32[]{:S(2)}, u32[]{:S(2)}) collective-permute-start(f32[256,1024]{1,0:T(8,128)} %get-tuple-element.114), channel_id=1, source_target_pairs={{0,2},{1,3},{2,0},{3,1},{4,6},{5,7},{6,4},{7,5},{8,10},{9,11},{10,... | collective-permute-start | bytes 3145736 | tf_op jit(solution)/shard_map/ppermute | solution.py:168
  359.0 19.8 %collective-permute-start.34 = (f32[128,256]{1,0:T(8,128)S(1)}, f32[128,256]{1,0:T(8,128)S(1)}, u32[]{:S(2)}, u32[]{:S(2)}) collective-permute-start(f32[128,256]{1,0:T(8,128)S(1)} %constant_dynamic-slice_fusion.4), channel_id=1, source_target_pairs={{0,16},{4,20},{8,24},{12,28},{16,0},{20,4},{24,8},{28,12},{1,17},{... | collective-permute-start | bytes 393224 | tf_op jit(solution)/shard_map/ppermute | solution.py:445
  361.7 28.9 %collective-permute-start.20 = (f32[256,1024]{1,0:T(8,128)}, f32[256,1024]{1,0:T(8,128)}, u32[]{:S(2)}, u32[]{:S(2)}) collective-permute-start(f32[256,1024]{1,0:T(8,128)} %get-tuple-element.114), channel_id=1, source_target_pairs={{0,1},{1,0},{2,3},{3,2},{4,5},{5,4},{6,7},{7,6},{8,9},{9,8},{10,11... | collective-permute-start | bytes 3145736 | tf_op jit(solution)/shard_map/ppermute | solution.py:164
  370.9 17.9 %collective-permute-start.25 = (f32[128,768]{1,0:T(8,128)}, f32[128,768]{1,0:T(8,128)}, u32[]{:S(2)}, u32[]{:S(2)}) collective-permute-start(f32[128,768]{1,0:T(8,128)} %constant_dynamic-slice_fusion.7), channel_id=1, source_target_pairs={{0,16},{4,20},{8,24},{12,28},{16,0},{20,4},{24,8},{28,12},{1,17},{... | collective-permute-start | bytes 1179656 | tf_op jit(solution)/shard_map/ppermute | solution.py:210
  378.2 16.9 %collective-permute-start.22 = (f32[256,1024]{1,0:T(8,128)}, f32[256,1024]{1,0:T(8,128)}, u32[]{:S(2)}, u32[]{:S(2)}) collective-permute-start(f32[256,1024]{1,0:T(8,128)} %collective-permute-done.21), channel_id=1, source_target_pairs={{0,1},{1,0},{2,3},{3,2},{4,5},{5,4},{6,7},{7,6},{8,9},{9,8},{10,11... | collective-permute-start | bytes 3145736 | tf_op jit(solution)/shard_map/ppermute | solution.py:164
  (77 other events, 528.9 us)
